TPU v7x, 32 devices: a whole 2x2x4 slice. The times are simulated.
32 devices in a mesh: ctx: 4 (over z), head: 4 (over y, x), fsdp: 2 (over core).
Axes of the slice: x: 2, y: 2, z: 4, core: 2. Of those that a mesh axis runs over, the one named last changes fastest.
Arguments:
- query_rows: bfloat16 [4096, 6144], P(('ctx', 'head'), 'fsdp'), may hold values from -400 to 400
- key_rows: bfloat16 [4096, 6144], P(('ctx', 'head'), 'fsdp'), may hold values from -8 to 8
- value_rows: bfloat16 [4096, 4096], P(('ctx', 'head'), 'fsdp'), may hold values from -6 to 6
- query_weight: bfloat16 [1536, 6144], P(('ctx', 'fsdp'), 'head'), may hold values from -6 to 6
- key_weight: bfloat16 [512, 4096], P(('ctx', 'fsdp'), 'head'), may hold values from -6 to 6
Outputs:
- attended: bfloat16 [4096, 4096], P('ctx', ('fsdp', 'head'))
- clipped_query: bfloat16 [1536, 6144], P(('ctx', 'fsdp'), 'head')
- clipped_key: bfloat16 [512, 4096], P(('ctx', 'fsdp'), 'head')
All inputs are finite; a program needn't handle non-finite values.
Results may differ from a plain program's by a relative error of at most 0.0033.
Values may be sent and summed in bfloat16 or wider, within the bound.
No kernel may reach another device: no remote copies, remote signals or barrier semaphores. Data moves between devices by JAX's collectives and lax.ppermute only.
A program may use at most 128 MiB of HBM per device.

v0:
```python
import jax
import jax.numpy as jnp
from jax import lax
from jax.sharding import PartitionSpec as P

DNOPE = 128
DROPE = 64
DV = 128
DQK = 192
clip_threshold = 100.0


def shifted_2(value, axis, steps):
    count = lax.axis_size(axis)
    first, last = (max(0, -steps), min(count, count - steps))
    return lax.ppermute(value, axis, [(source, source + steps) for source in range(first, last)])


def partial_softmax(scores, value_cube):
    highest = jnp.max(scores, axis=2)
    present = jnp.isfinite(highest)
    shifted = jnp.where(present, highest, 0.0)
    weights = jnp.exp(scores - shifted[:, :, None])
    totals = jnp.sum(weights, axis=2)
    rounded = weights.astype(jnp.bfloat16)
    summed = jnp.einsum("htu,uhd->thd", rounded, value_cube, preferred_element_type=jnp.float32)
    return (summed, totals, jnp.where(present, highest, -jnp.inf))


def merge_parts(own_part, far_part):
    own_sum, own_total, own_high = own_part
    far_sum, far_total, far_high = far_part
    highest = jnp.maximum(own_high, far_high)
    own_scale = jnp.exp(own_high - highest)
    far_scale = jnp.exp(far_high - highest)
    totals = own_total * own_scale + far_total * far_scale
    mixed = own_sum * own_scale.T[:, :, None] + far_sum * far_scale.T[:, :, None]
    return mixed / totals.T[:, :, None]


def head_scores(query_cube, key_cube):
    return jnp.einsum(
        "thd,uhd->htu", query_cube, key_cube, preferred_element_type=jnp.float32
    ) * DQK ** (-0.5)


def causal_block(query_cube, key_cube, value_cube, row_start, block_rows):
    row_count = key_cube.shape[0]
    query_block = query_cube[row_start : row_start + block_rows]
    row_ids = lax.broadcasted_iota(jnp.int32, (block_rows, row_count), 0) + row_start
    col_ids = lax.broadcasted_iota(jnp.int32, (block_rows, row_count), 1)
    scores = jnp.where((row_ids >= col_ids)[None], head_scores(query_block, key_cube), -jnp.inf)
    return (partial_softmax(scores, value_cube), jnp.max(scores, axis=(1, 2)))


def body(query_rows, key_rows, value_rows, query_weight, key_weight):
    local_query, local_key, local_value = (
        lax.all_to_all(query_rows, "head", split_axis=1, concat_axis=0, tiled=True),
        lax.all_to_all(key_rows, "head", split_axis=1, concat_axis=0, tiled=True),
        lax.all_to_all(value_rows, "head", split_axis=1, concat_axis=0, tiled=True),
    )
    row_count = local_query.shape[0]
    head_count = local_query.shape[1] // DQK
    query_cube = local_query.reshape(row_count, head_count, DQK)
    key_cube = local_key.reshape(row_count, head_count, DQK)
    value_cube = local_value.reshape(row_count, head_count, DV)
    block_index = lax.axis_index("ctx")
    block_rows = min(512, row_count)
    row_starts = list(range(0, row_count, block_rows))
    local_peak = jnp.full((head_count,), -jnp.inf, jnp.float32)
    pieces = []
    far_key, far_value = shifted_2((local_key, local_value), "ctx", 1)
    far_keys = far_key.reshape(row_count, head_count, DQK)
    far_values = far_value.reshape(row_count, head_count, DV)
    for row_start in row_starts:
        own_part, own_peak = causal_block(query_cube, key_cube, value_cube, row_start, block_rows)
        far_scores = jnp.where(
            block_index > 0,
            head_scores(query_cube[row_start : row_start + block_rows], far_keys),
            -jnp.inf,
        )
        far_part = partial_softmax(far_scores, far_values)
        local_peak = jnp.maximum(
            local_peak, jnp.maximum(own_peak, jnp.max(far_scores, axis=(1, 2)))
        )
        pieces.append(merge_parts(own_part, far_part))
    attended = (
        jnp.concatenate(pieces, axis=0).astype(jnp.bfloat16).reshape(row_count, head_count * DV)
    )
    weight_heads = key_weight.shape[1] // DNOPE
    cycle_peak = lax.pmax(local_peak, "ctx")
    gathered = lax.all_gather(cycle_peak, ("head", "fsdp"), axis=0, tiled=True)
    head_peak = (
        gathered.reshape(lax.axis_size("head"), lax.axis_size("fsdp"), head_count)
        .transpose(1, 0, 2)
        .reshape(-1)
    )
    own_peaks = lax.dynamic_slice_in_dim(
        head_peak, lax.axis_index("head") * weight_heads, weight_heads, 0
    )
    factor = jnp.minimum(1.0, clip_threshold / own_peaks)
    root_factor = jnp.sqrt(factor)
    column_factor = jnp.concatenate(
        [
            jnp.broadcast_to(root_factor[:, None], (weight_heads, DNOPE)),
            jnp.broadcast_to(factor[:, None], (weight_heads, DROPE)),
        ],
        axis=1,
    )
    query_count = query_weight.shape[0]
    key_count = key_weight.shape[0]
    clipped_query = (
        (
            query_weight.astype(jnp.float32).reshape(query_count, weight_heads, DQK)
            * column_factor[None]
        )
        .astype(jnp.bfloat16)
        .reshape(query_count, weight_heads * DQK)
    )
    clipped_key = (
        (
            key_weight.astype(jnp.float32).reshape(key_count, weight_heads, DNOPE)
            * root_factor[None, :, None]
        )
        .astype(jnp.bfloat16)
        .reshape(key_count, weight_heads * DNOPE)
    )
    return (attended, clipped_query, clipped_key)


def solution(mesh):
    return jax.shard_map(
        body,
        mesh=mesh,
        in_specs=(
            P(("ctx", "head"), "fsdp"),
            P(("ctx", "head"), "fsdp"),
            P(("ctx", "head"), "fsdp"),
            P(("ctx", "fsdp"), "head"),
            P(("ctx", "fsdp"), "head"),
        ),
        out_specs=(
            P("ctx", ("fsdp", "head")),
            P(("ctx", "fsdp"), "head"),
            P(("ctx", "fsdp"), "head"),
        ),
        check_vma=False,
    )
```

profile of v0, /device:TPU:0, one launch (start us, length us, event | category | flops | bytes accessed | tf_op | source)
XLA Modules:
  0.0 180.5 jit_solution(10534738147140960069)
XLA Ops:
  0.6 2.3 %copy.29 = bf16[256,2048]{0,1:T(8,128)(2,1)} copy(bf16[256,2048]{1,0:T(8,128)(2,1)} %param.7) | data formatting | bytes 2097152 | tf_op args[2]
  2.9 5.2 %all-to-all-start.2 = ((bf16[256,4,512]{0,2,1:T(8,128)(2,1)}), bf16[256,4,512]{0,2,1:T(8,128)(2,1)S(1)}, u32[]{:S(2)}, u32[]{:S(2)}) async-start(bf16[256,4,512]{0,2,1:T(8,128)(2,1)} %bitcast.5), calls=%async_computation.2 | async-start | bytes 2097152 | tf_op jit(solution)/shard_map/all_to_all | solution.py:60
  8.1 2.6 %copy.26 = bf16[256,3072]{0,1:T(8,128)(2,1)} copy(bf16[256,3072]{1,0:T(8,128)(2,1)} %param.6) | data formatting | bytes 3145728 | tf_op args[1]
  10.7 11.0 %all-to-all-done.2 = bf16[256,4,512]{0,2,1:T(8,128)(2,1)S(1)} async-done(((bf16[256,4,512]{0,2,1:T(8,128)(2,1)}), bf16[256,4,512]{0,2,1:T(8,128)(2,1)S(1)}, u32[]{:S(2)}, u32[]{:S(2)}) %all-to-all-start.2) | async-done | bytes 1048608 | tf_op jit(solution)/shard_map/all_to_all | solution.py:60
  21.7 3.6 %all-to-all-start.1 = ((bf16[256,4,768]{0,2,1:T(8,128)(2,1)}), bf16[256,4,768]{0,2,1:T(8,128)(2,1)S(1)}, u32[]{:S(2)}, u32[]{:S(2)}) async-start(bf16[256,4,768]{0,2,1:T(8,128)(2,1)} %bitcast.115), calls=%async_computation.1 | async-start | bytes 3145728 | tf_op jit(solution)/shard_map/all_to_all | solution.py:59
  25.3 2.6 %copy.24 = bf16[256,3072]{0,1:T(8,128)(2,1)} copy(bf16[256,3072]{1,0:T(8,128)(2,1)} %param.5) | data formatting | bytes 3145728 | tf_op args[0]
  27.9 16.1 %all-to-all-done.1 = bf16[256,4,768]{0,2,1:T(8,128)(2,1)S(1)} async-done(((bf16[256,4,768]{0,2,1:T(8,128)(2,1)}), bf16[256,4,768]{0,2,1:T(8,128)(2,1)S(1)}, u32[]{:S(2)}, u32[]{:S(2)}) %all-to-all-start.1) | async-done | bytes 1572896 | tf_op jit(solution)/shard_map/all_to_all | solution.py:59
  44.0 4.3 %all-to-all-start = ((bf16[256,4,768]{0,2,1:T(8,128)(2,1)}), bf16[256,4,768]{0,2,1:T(8,128)(2,1)}, u32[]{:S(2)}, u32[]{:S(2)}) async-start(bf16[256,4,768]{0,2,1:T(8,128)(2,1)} %bitcast.114), calls=%async_computation | async-start | bytes 3145728 | tf_op jit(solution)/shard_map/all_to_all | solution.py:58
  51.8 1.8 copy.31
  53.6 2.6 %reshape.100 = bf16[1024,4,128]{0,2,1:T(8,128)(2,1)} reshape(bf16[4,256,512]{1,0,2:T(4,128)(2,1)} %copy.31) | data formatting | bytes 2097152 | tf_op jit(solution)/shard_map/reshape | solution.py:66
  57.4 4.5 %collective-permute-start.1 = (bf16[1024,512]{1,0:T(8,128)(2,1)}, bf16[1024,512]{1,0:T(8,128)(2,1)}, u32[]{:S(2)}, u32[]{:S(2)}) collective-permute-start(bf16[1024,512]{1,0:T(8,128)(2,1)} %bitcast.118), channel_id=1, source_target_pairs={{0,8},{8,16},{16,24},{1,9},{9,17},{17,25},{2,10},{10,18},{18,26},{... | collective-permute-start | bytes 3145736 | tf_op jit(solution)/shard_map/ppermute | solution.py:16
  63.6 3.6 %collective-permute-start = (bf16[1024,768]{1,0:T(8,128)(2,1)}, bf16[1024,768]{1,0:T(8,128)(2,1)}, u32[]{:S(2)}, u32[]{:S(2)}) collective-permute-start(bf16[1024,768]{1,0:T(8,128)(2,1)} %bitcast.10), channel_id=1, source_target_pairs={{0,8},{8,16},{16,24},{1,9},{9,17},{17,25},{2,10},{10,18},{18,26},{... | collective-permute-start | bytes 4718600 | tf_op jit(solution)/shard_map/ppermute | solution.py:16
  74.3 2.5 %reshape.99 = bf16[1024,4,192]{0,2,1:T(8,128)(2,1)} reshape(bf16[4,256,768]{1,0,2:T(4,128)(2,1)S(1)} %copy.28) | data formatting | bytes 3145728 | tf_op jit(solution)/shard_map/reshape | solution.py:65
  76.8 3.8 %fusion.13 = (f32[4,512]{1,0:T(4,128)S(1)}, f32[4,512,1024]{2,1,0:T(8,128)S(1)}) fusion(pred[512,1024]{1,0:T(8,128)(4,1)} %iota_compare_fusion, bf16[512,4,192]{0,2,1:T(8,128)(2,1)} %slice.17, bf16[1024,4,192]{0,2,1:T(8,128)(2,1)} %reshape.99), kind=kOutput, calls=%fused_computation.21 | convolution fusion | flops 811595776 | bytes 11280384 | tf_op jit(solution)/shard_map/thd,uhd->htu/dot_general | solution.py:42
  80.7 1.9 %fusion.9 = (f32[4,512]{1,0:T(4,128)S(1)}, f32[4,512,1024]{2,1,0:T(8,128)S(1)}) fusion(pred[512,1024]{1,0:T(8,128)(4,1)S(1)} %copy-done.5, bf16[512,4,192]{0,2,1:T(8,128)(2,1)S(1)} %copy-done.9, bf16[1024,4,192]{0,2,1:T(8,128)(2,1)S(1)} %copy-done.6), kind=kOutput, calls=%fused_computation.17 | convolution fusion | flops 811595776 | bytes 11280384 | tf_op jit(solution)/shard_map/thd,uhd->htu/dot_general | solution.py:42
  82.7 5.6 %fusion.8 = (f32[4]{0:T(128)S(1)}, f32[4,512]{1,0:T(4,128)S(1)}, f32[4,512]{1,0:T(4,128)S(1)}, f32[4]{0:T(128)S(1)}) fusion(f32[4,512,1024]{2,1,0:T(8,128)S(1)} %get-tuple-element.26, pred[512,1024]{1,0:T(8,128)(4,1)S(1)} %copy-done.5, f32[4,512]{1,0:T(4,128)S(1)} %is-finite_select_fusion.7, f32[4,512]{1,0:T(4,128)S(1)} %is-finite_select_fusion.3, ...), kind=kLoop, calls=%fused_computation.16 | loop fusion | flops 20967416 | bytes 17858592 | tf_op jit(solution)/shard_map/reduce_max | solution.py:53
  88.3 28.4 %collective-permute-done = bf16[1024,768]{1,0:T(8,128)(2,1)} collective-permute-done((bf16[1024,768]{1,0:T(8,128)(2,1)}, bf16[1024,768]{1,0:T(8,128)(2,1)}, u32[]{:S(2)}, u32[]{:S(2)}) %collective-permute-start) | collective-permute-done | bytes 1572896 | tf_op jit(solution)/shard_map/ppermute | solution.py:16
  121.5 4.6 %fusion.10 = (f32[4]{0:T(128)S(1)}, f32[4,512]{1,0:T(4,128)S(1)}, f32[4,512]{1,0:T(4,128)S(1)}, f32[4]{0:T(128)S(1)}) fusion(f32[4,512,1024]{2,1,0:T(8,128)S(1)} %get-tuple-element.28, pred[]{:T(512)S(6)} %gt.4, f32[4,512]{1,0:T(4,128)S(1)} %is-finite_select_fusion.4, f32[4,512]{1,0:T(4,128)S(1)} %is-finite_select_fusion, ...), kind=kLoop, calls=%fused_computation.18 | loop fusion | flops 20967416 | bytes 16810016 | tf_op jit(solution)/shard_map/reduce_max | solution.py:84
  127.6 12.9 %pmax.7 = f32[4]{0:T(128)S(1)} all-reduce(f32[4]{0:T(128)S(1)} %maximum_maximum_fusion), channel_id=1, replica_groups=mesh['ctx'=4,'head'=4,'fsdp'=2] {'ctx'}, use_global_device_ids=true, to_apply=%region_12.13 | all-reduce | flops 4 | bytes 32 | tf_op jit(solution)/shard_map/pmax | solution.py:91
  140.8 12.0 %all-reduce.1 = f32[32]{0:T(128)S(1)} all-reduce(f32[32]{0:T(128)S(1)} %reshape.104), channel_id=1, replica_groups=mesh['ctx'=4,'head'=4,'fsdp'=2] {'head','fsdp'}, use_global_device_ids=true, to_apply=%add | all-reduce | flops 32 | bytes 256
  153.3 4.7 %fusion.49 = f32[512,4,128]{0,2,1:T(8,128)S(1)} fusion(bf16[1024,4,128]{0,2,1:T(8,128)(2,1)S(1)} %copy-done.7, f32[4,512,1024]{2,1,0:T(8,128)} %copy-done.3, f32[4,512]{1,0:T(4,128)S(1)} %is-finite_select_fusion.7, pred[512,1024]{1,0:T(8,128)(4,1)S(1)} %copy-done.5, f32[512,4]{0,1:T(4,128)S(1)} %get-tuple-element.15), kind=kOutput, calls=%fused_computation.41 | convolution fusion | flops 545521664 | bytes 11026432 | tf_op jit(solution)/shard_map/htu,uhd->thd/dot_general | solution.py:26
  158.0 6.3 %divide_convert_fusion.1 = bf16[512,4,128]{0,2,1:T(8,128)(2,1)} fusion(f32[512,4,128]{0,2,1:T(8,128)S(1)} %fusion.49, bf16[1024,4,128]{0,2,1:T(8,128)(2,1)S(1)} %bitcast.119, f32[4,512,1024]{2,1,0:T(8,128)} %copy-done.1, f32[4,512]{1,0:T(4,128)S(1)} %is-finite_select_fusion.4, pred[]{:T(512)S(6)} %gt.4, f32[512,4]{0,1:T(4,128)S(1)} %get-tuple-element.13, ...), kind=kOutput, calls=%fused_computation.47 | convolution fusion | flops 546308096 | bytes 11034625 | tf_op jit(solution)/shard_map/htu,uhd->thd/dot_general | solution.py:26
  165.5 4.7 %fusion.46 = f32[512,4,128]{0,2,1:T(8,128)S(1)} fusion(bf16[1024,4,128]{0,2,1:T(8,128)(2,1)S(1)} %copy-done.7, f32[4,512,1024]{2,1,0:T(8,128)} %copy-done.2, f32[4,512]{1,0:T(4,128)S(1)} %is-finite_select_fusion.3, pred[512,1024]{1,0:T(8,128)(4,1)S(1)} %copy-done.4, f32[512,4]{0,1:T(4,128)S(1)} %get-tuple-element.18), kind=kOutput, calls=%fused_computation.40 | convolution fusion | flops 545521664 | bytes 11026432 | tf_op jit(solution)/shard_map/htu,uhd->thd/dot_general | solution.py:26
  170.2 6.3 %divide_convert_fusion = bf16[512,4,128]{0,2,1:T(8,128)(2,1)} fusion(f32[512,4,128]{0,2,1:T(8,128)S(1)} %fusion.46, bf16[1024,4,128]{0,2,1:T(8,128)(2,1)S(1)} %bitcast.120, f32[4,512,1024]{2,1,0:T(8,128)} %copy-done, f32[4,512]{1,0:T(4,128)S(1)} %is-finite_select_fusion, pred[]{:T(512)S(6)} %gt.4, f32[512,4]{0,1:T(4,128)S(1)} %get-tuple-element.16, ...), kind=kOutput, calls=%fused_computation.46 | convolution fusion | flops 546308096 | bytes 11034625 | tf_op jit(solution)/shard_map/htu,uhd->thd/dot_general | solution.py:26
  (69 shorter events, 25.0 us)
Async XLA Ops:
  0.6 47.8 %copy-start.13 = (u32[32]{0:T(128)S(1)}, u32[32]{0:T(128)}, u32[]{:S(2)}) copy-start(u32[32]{0:T(128)} %constant.30) | copy-start | bytes 388
  2.9 18.8 %all-to-all-start.2 = ((bf16[256,4,512]{0,2,1:T(8,128)(2,1)}), bf16[256,4,512]{0,2,1:T(8,128)(2,1)S(1)}, u32[]{:S(2)}, u32[]{:S(2)}) async-start(bf16[256,4,512]{0,2,1:T(8,128)(2,1)} %bitcast.5), calls=%async_computation.2 | async-start | bytes 2097152 | tf_op jit(solution)/shard_map/all_to_all | solution.py:60
  21.7 22.3 %all-to-all-start.1 = ((bf16[256,4,768]{0,2,1:T(8,128)(2,1)}), bf16[256,4,768]{0,2,1:T(8,128)(2,1)S(1)}, u32[]{:S(2)}, u32[]{:S(2)}) async-start(bf16[256,4,768]{0,2,1:T(8,128)(2,1)} %bitcast.115), calls=%async_computation.1 | async-start | bytes 3145728 | tf_op jit(solution)/shard_map/all_to_all | solution.py:59
  44.0 23.2 %all-to-all-start = ((bf16[256,4,768]{0,2,1:T(8,128)(2,1)}), bf16[256,4,768]{0,2,1:T(8,128)(2,1)}, u32[]{:S(2)}, u32[]{:S(2)}) async-start(bf16[256,4,768]{0,2,1:T(8,128)(2,1)} %bitcast.114), calls=%async_computation | async-start | bytes 3145728 | tf_op jit(solution)/shard_map/all_to_all | solution.py:58
  57.4 68.6 %collective-permute-start.1 = (bf16[1024,512]{1,0:T(8,128)(2,1)}, bf16[1024,512]{1,0:T(8,128)(2,1)}, u32[]{:S(2)}, u32[]{:S(2)}) collective-permute-start(bf16[1024,512]{1,0:T(8,128)(2,1)} %bitcast.118), channel_id=1, source_target_pairs={{0,8},{8,16},{16,24},{1,9},{9,17},{17,25},{2,10},{10,18},{18,26},{... | collective-permute-start | bytes 3145736 | tf_op jit(solution)/shard_map/ppermute | solution.py:16
  63.6 53.1 %collective-permute-start = (bf16[1024,768]{1,0:T(8,128)(2,1)}, bf16[1024,768]{1,0:T(8,128)(2,1)}, u32[]{:S(2)}, u32[]{:S(2)}) collective-permute-start(bf16[1024,768]{1,0:T(8,128)(2,1)} %bitcast.10), channel_id=1, source_target_pairs={{0,8},{8,16},{16,24},{1,9},{9,17},{17,25},{2,10},{10,18},{18,26},{... | collective-permute-start | bytes 4718600 | tf_op jit(solution)/shard_map/ppermute | solution.py:16
  74.3 6.3 %copy-start.5 = (pred[512,1024]{1,0:T(8,128)(4,1)S(1)}, pred[512,1024]{1,0:T(8,128)(4,1)}, u32[]{:S(2)}) copy-start(pred[512,1024]{1,0:T(8,128)(4,1)} %iota_compare_fusion.1) | copy-start | bytes 1572868
  76.8 3.8 %copy-start.6 = (bf16[1024,4,192]{0,2,1:T(8,128)(2,1)S(1)}, bf16[1024,4,192]{0,2,1:T(8,128)(2,1)}, u32[]{:S(2)}) copy-start(bf16[1024,4,192]{0,2,1:T(8,128)(2,1)} %reshape.99) | copy-start | bytes 4718596
  76.8 3.8 %copy-start.9 = (bf16[512,4,192]{0,2,1:T(8,128)(2,1)S(1)}, bf16[512,4,192]{0,2,1:T(8,128)(2,1)}, u32[]{:S(2)}) copy-start(bf16[512,4,192]{0,2,1:T(8,128)(2,1)} %slice.15) | copy-start | bytes 2359300
  80.7 7.6 %copy-start.2 = (f32[4,512,1024]{2,1,0:T(8,128)}, f32[4,512,1024]{2,1,0:T(8,128)S(1)}, u32[]{:S(2)}) copy-start(f32[4,512,1024]{2,1,0:T(8,128)S(1)} %get-tuple-element.22) | copy-start | bytes 25165828
  80.7 2.0 %copy-start.4 = (pred[512,1024]{1,0:T(8,128)(4,1)S(1)}, pred[512,1024]{1,0:T(8,128)(4,1)}, u32[]{:S(2)}) copy-start(pred[512,1024]{1,0:T(8,128)(4,1)} %iota_compare_fusion) | copy-start | bytes 1572868
  82.6 5.7 %copy-start.3 = (f32[4,512,1024]{2,1,0:T(8,128)}, f32[4,512,1024]{2,1,0:T(8,128)S(1)}, u32[]{:S(2)}) copy-start(f32[4,512,1024]{2,1,0:T(8,128)S(1)} %get-tuple-element.26) | copy-start | bytes 25165828
  82.6 35.7 %copy-start.8 = (bf16[512,4,192]{0,2,1:T(8,128)(2,1)S(1)}, bf16[512,4,192]{0,2,1:T(8,128)(2,1)}, u32[]{:S(2)}) copy-start(bf16[512,4,192]{0,2,1:T(8,128)(2,1)} %slice.17) | copy-start | bytes 2359300
  118.3 1.5 copy-start.10
  119.9 6.1 %copy-start = (f32[4,512,1024]{2,1,0:T(8,128)}, f32[4,512,1024]{2,1,0:T(8,128)S(1)}, u32[]{:S(2)}) copy-start(f32[4,512,1024]{2,1,0:T(8,128)S(1)} %get-tuple-element.24) | copy-start | bytes 25165828
  121.4 4.6 %copy-start.1 = (f32[4,512,1024]{2,1,0:T(8,128)}, f32[4,512,1024]{2,1,0:T(8,128)S(1)}, u32[]{:S(2)}) copy-start(f32[4,512,1024]{2,1,0:T(8,128)S(1)} %get-tuple-element.28) | copy-start | bytes 25165828
  121.5 31.8 %copy-start.7 = (bf16[1024,4,128]{0,2,1:T(8,128)(2,1)S(1)}, bf16[1024,4,128]{0,2,1:T(8,128)(2,1)}, u32[]{:S(2)}) copy-start(bf16[1024,4,128]{0,2,1:T(8,128)(2,1)} %reshape.100) | copy-start | bytes 3145732
  170.2 7.6 %copy-start.11 = (bf16[192,1536]{1,0:T(8,128)(2,1)S(1)}, bf16[192,1536]{1,0:T(8,128)(2,1)}, u32[]{:S(2)}) copy-start(bf16[192,1536]{1,0:T(8,128)(2,1)} %param.8) | copy-start | bytes 1769476
  170.2 8.5 %copy-start.12 = (bf16[64,1024]{1,0:T(8,128)(2,1)S(1)}, bf16[64,1024]{1,0:T(8,128)(2,1)}, u32[]{:S(2)}) copy-start(bf16[64,1024]{1,0:T(8,128)(2,1)} %param.9) | copy-start | bytes 393220
where the time goes:
time: 181 us; the launch traced here: 180 us
  waiting for transfers between devices  55.5 us (31%)
  local copies, waits for them, and re-layouts  31.4 us (17%)
  matrix products  30.7 us (17%)
  blocking collectives  24.9 us (14%)
  starting transfers between devices  21.2 us (12%)
  other arithmetic  15.1 us (8%)
    ppermute x2, waiting for transfers between devices, shifted_2(): lax.ppermute(value, axis, [(source, source + steps) for source in range(f...  28.4 us
    dot_general x4, matrix products, partial_softmax(): jnp.einsum('htu,uhd->thd', rounded, value_cube, preferred_element_type=jn...  22 us
    all_to_all x1, waiting for transfers between devices, body(): lax.all_to_all(key_rows, 'head', split_axis=1, concat_axis=0, tiled=True)  16.1 us
    pmax x1, blocking collectives, body(): cycle_peak = lax.pmax(local_peak, 'ctx')  12.9 us
    unnamed x1, blocking collectives  12 us
    all_to_all x1, waiting for transfers between devices, body(): lax.all_to_all(value_rows, 'head', split_axis=1, concat_axis=0, tiled=True)  11 us
    dot_general x4, matrix products, head_scores(): jnp.einsum('thd,uhd->htu', query_cube, key_cube, preferred_element_type=j...  8.76 us
    unnamed x34, local copies, waits for them, and re-layouts  8.34 us
  transfers between devices with their start and end apart: 5, of which 3 were waited for; matrix products, arithmetic and copies ran while one was open for 25% of the time, Pallas kernels for 0%

commit v1 on v0

--- a/solution.py
+++ b/solution.py
@@ -8,6 +8,18 @@
 DV = 128
 DQK = 192
 clip_threshold = 100.0
+
+
+def return_all_bands_for(inputs, named_axis, ndim_at, pos_dim=0):
+    return jnp.concatenate(
+        jax.lax.all_to_all(
+            jnp.stack(jnp.split(inputs, jax.lax.axis_size(named_axis), axis=ndim_at)),
+            named_axis,
+            0,
+            0,
+        ),
+        axis=pos_dim,
+    )
 
 
 def shifted_2(value, axis, steps):
@@ -57,7 +69,7 @@
     local_query, local_key, local_value = (
         lax.all_to_all(query_rows, "head", split_axis=1, concat_axis=0, tiled=True),
         lax.all_to_all(key_rows, "head", split_axis=1, concat_axis=0, tiled=True),
-        lax.all_to_all(value_rows, "head", split_axis=1, concat_axis=0, tiled=True),
+        return_all_bands_for(value_rows, "head", ndim_at=1),
     )
     row_count = local_query.shape[0]
     head_count = local_query.shape[1] // DQK

time: 181 us -> 172 us (0.950)
  waiting for transfers between devices: 55.5 us -> 38.2 us
  blocking collectives: 24.9 us -> 38.2 us
  local copies, waits for them, and re-layouts: 31.4 us -> 26.9 us
  matrix products: 30.7 us -> 27.6 us
  starting transfers between devices: 21.2 us -> 23.2 us
    ppermute x2, waiting for transfers between devices: 28.4 us -> 6.63 us  [shifted_2(): lax.ppermute(value, axis, [(source, source + steps) for source in range(f...]
    pmax x1, blocking collectives: 12.9 us -> 26.2 us  [body(): cycle_peak = lax.pmax(local_peak, 'ctx')]
    another operation x0 -> x3, local copies, waits for them, and re-layouts: none -> 4.79 us  [the longest x2 3.53 us: body(): value_cube = local_value.reshape(row_count, head_count, DV)]
    all_to_all x1, waiting for transfers between devices: 0.01 us -> 4.35 us  [body(): lax.all_to_all(query_rows, 'head', split_axis=1, concat_axis=0, tiled=True)]
    dot_general x4, matrix products: 22 us -> 18.8 us  [partial_softmax(): jnp.einsum('htu,uhd->thd', rounded, value_cube, preferred_element_type=jn...]
    all_to_all x2 -> x0, local copies, waits for them, and re-layouts: 3.09 us -> none  [body(): lax.all_to_all(value_rows, 'head', split_axis=1, concat_axis=0, tiled=True)]
    concatenate x2, local copies, waits for them, and re-layouts: 2.5 us -> 0.43 us  [body(): jnp.concatenate(pieces, axis=0).astype(jnp.bfloat16)]
    ppermute x2, starting transfers between devices: 8.16 us -> 10.1 us  [shifted_2(): lax.ppermute(value, axis, [(source, source + steps) for source in range(f...]
  transfers between devices with their start and end apart: 5 -> 5, of which waited for: 3 -> 4; matrix products, arithmetic and copies ran while one was open for 25% -> 24% of each run, Pallas kernels for 0% -> 0%
where the time goes in v1:
time: 172 us
  waiting for transfers between devices  38.2 us (22%)
  blocking collectives  38.2 us (22%)
  matrix products  27.6 us (16%)
  local copies, waits for them, and re-layouts  26.9 us (16%)
  starting transfers between devices  23.2 us (13%)
  other arithmetic  16.2 us (9%)
    pmax x1, blocking collectives, body(): cycle_peak = lax.pmax(local_peak, 'ctx')  26.2 us
    dot_general x4, matrix products, partial_softmax(): jnp.einsum('htu,uhd->thd', rounded, value_cube, preferred_element_type=jn...  18.8 us
    all_to_all x1, waiting for transfers between devices, body(): lax.all_to_all(key_rows, 'head', split_axis=1, concat_axis=0, tiled=True)  16.1 us
    unnamed x1, blocking collectives  12 us
    all_to_all x1, waiting for transfers between devices, return_all_bands_for(): jax.lax.all_to_all(jnp.stack(jnp.split(inputs, jax.lax.axis_size(named_ax...  11 us
    ppermute x2, starting transfers between devices, shifted_2(): lax.ppermute(value, axis, [(source, source + steps) for source in range(f...  10.1 us
    dot_general x4, matrix products, head_scores(): jnp.einsum('thd,uhd->htu', query_cube, key_cube, preferred_element_type=j...  8.76 us
    unnamed x37, local copies, waits for them, and re-layouts  7.07 us
  transfers between devices with their start and end apart: 5, of which 4 were waited for; matrix products, arithmetic and copies ran while one was open for 24% of the time, Pallas kernels for 0%

profile of v1, /device:TPU:0, one launch (start us, length us, event | category | flops | bytes accessed | tf_op | source)
XLA Modules:
  0.0 171.8 jit_solution(17447646202404038495)
XLA Ops:
  3.0 5.2 %all-to-all-start = ((bf16[4,256,512]{2,1,0:T(8,128)(2,1)}), bf16[4,256,512]{2,1,0:T(8,128)(2,1)S(1)}, u32[]{:S(2)}, u32[]{:S(2)}) async-start(bf16[4,256,512]{2,1,0:T(8,128)(2,1)} %pad_maximum_fusion), calls=%async_computation | async-start | bytes 2097152 | tf_op jit(solution)/shard_map/all_to_all | solution.py:15
  8.2 2.6 %copy.28 = bf16[256,3072]{0,1:T(8,128)(2,1)} copy(bf16[256,3072]{1,0:T(8,128)(2,1)} %param.6) | data formatting | bytes 3145728 | tf_op args[1]
  10.8 11.0 %all-to-all-done = bf16[4,256,512]{2,1,0:T(8,128)(2,1)S(1)} async-done(((bf16[4,256,512]{2,1,0:T(8,128)(2,1)}), bf16[4,256,512]{2,1,0:T(8,128)(2,1)S(1)}, u32[]{:S(2)}, u32[]{:S(2)}) %all-to-all-start) | async-done | bytes 1048608 | tf_op jit(solution)/shard_map/all_to_all | solution.py:15
  21.8 3.6 %all-to-all-start.2 = ((bf16[256,4,768]{0,2,1:T(8,128)(2,1)}), bf16[256,4,768]{0,2,1:T(8,128)(2,1)S(1)}, u32[]{:S(2)}, u32[]{:S(2)}) async-start(bf16[256,4,768]{0,2,1:T(8,128)(2,1)} %bitcast.117), calls=%async_computation.2 | async-start | bytes 3145728 | tf_op jit(solution)/shard_map/all_to_all | solution.py:71
  25.4 2.6 %copy.26 = bf16[256,3072]{0,1:T(8,128)(2,1)} copy(bf16[256,3072]{1,0:T(8,128)(2,1)} %param.5) | data formatting | bytes 3145728 | tf_op args[0]
  28.0 16.1 %all-to-all-done.2 = bf16[256,4,768]{0,2,1:T(8,128)(2,1)S(1)} async-done(((bf16[256,4,768]{0,2,1:T(8,128)(2,1)}), bf16[256,4,768]{0,2,1:T(8,128)(2,1)S(1)}, u32[]{:S(2)}, u32[]{:S(2)}) %all-to-all-start.2) | async-done | bytes 1572896 | tf_op jit(solution)/shard_map/all_to_all | solution.py:71
  44.1 4.3 %all-to-all-start.1 = ((bf16[256,4,768]{0,2,1:T(8,128)(2,1)}), bf16[256,4,768]{0,2,1:T(8,128)(2,1)}, u32[]{:S(2)}, u32[]{:S(2)}) async-start(bf16[256,4,768]{0,2,1:T(8,128)(2,1)} %bitcast.116), calls=%async_computation.1 | async-start | bytes 3145728 | tf_op jit(solution)/shard_map/all_to_all | solution.py:70
  53.0 2.4 %copy.37 = bf16[1024,4,128]{0,2,1:T(8,128)(2,1)} copy(bf16[1024,4,128]{2,1,0:T(4,128)(2,1)} %reshape.106) | data formatting | bytes 2097152 | tf_op jit(solution)/shard_map/reshape;reshape | solution.py:78
  58.3 4.7 %collective-permute-start = (bf16[1024,768]{1,0:T(8,128)(2,1)}, bf16[1024,768]{1,0:T(8,128)(2,1)}, u32[]{:S(2)}, u32[]{:S(2)}) collective-permute-start(bf16[1024,768]{1,0:T(8,128)(2,1)} %bitcast.11), channel_id=1, source_target_pairs={{0,8},{8,16},{16,24},{1,9},{9,17},{17,25},{2,10},{10,18},{18,26},{... | collective-permute-start | bytes 4718600 | tf_op jit(solution)/shard_map/ppermute | solution.py:28
  63.0 4.3 %all-to-all-done.1 = bf16[256,4,768]{0,2,1:T(8,128)(2,1)} async-done(((bf16[256,4,768]{0,2,1:T(8,128)(2,1)}), bf16[256,4,768]{0,2,1:T(8,128)(2,1)}, u32[]{:S(2)}, u32[]{:S(2)}) %all-to-all-start.1) | async-done | bytes 1572896 | tf_op jit(solution)/shard_map/all_to_all | solution.py:70
  74.4 2.5 %reshape.95 = bf16[1024,4,192]{0,2,1:T(8,128)(2,1)} reshape(bf16[4,256,768]{1,0,2:T(4,128)(2,1)S(1)} %copy.30) | data formatting | bytes 3145728 | tf_op jit(solution)/shard_map/reshape | solution.py:77
  76.9 3.8 %fusion.13 = (f32[4,512]{1,0:T(4,128)S(1)}, f32[4,512,1024]{2,1,0:T(8,128)S(1)}) fusion(pred[512,1024]{1,0:T(8,128)(4,1)} %iota_compare_fusion, bf16[512,4,192]{0,2,1:T(8,128)(2,1)} %slice.17, bf16[1024,4,192]{0,2,1:T(8,128)(2,1)} %reshape.95), kind=kOutput, calls=%fused_computation.21 | convolution fusion | flops 811595776 | bytes 11280384 | tf_op jit(solution)/shard_map/thd,uhd->htu/dot_general | solution.py:54
  80.8 1.9 %fusion.9 = (f32[4,512]{1,0:T(4,128)S(1)}, f32[4,512,1024]{2,1,0:T(8,128)S(1)}) fusion(pred[512,1024]{1,0:T(8,128)(4,1)S(1)} %copy-done.6, bf16[512,4,192]{0,2,1:T(8,128)(2,1)S(1)} %copy-done.11, bf16[1024,4,192]{0,2,1:T(8,128)(2,1)S(1)} %copy-done.7), kind=kOutput, calls=%fused_computation.17 | convolution fusion | flops 811595776 | bytes 11280384 | tf_op jit(solution)/shard_map/thd,uhd->htu/dot_general | solution.py:54
  82.8 5.6 %fusion.8 = (f32[4]{0:T(128)S(1)}, f32[4,512]{1,0:T(4,128)S(1)}, f32[4,512]{1,0:T(4,128)S(1)}, f32[4]{0:T(128)S(1)}) fusion(f32[4,512,1024]{2,1,0:T(8,128)S(1)} %get-tuple-element.30, pred[512,1024]{1,0:T(8,128)(4,1)S(1)} %copy-done.6, f32[4,512]{1,0:T(4,128)S(1)} %is-finite_select_fusion.7, f32[4,512]{1,0:T(4,128)S(1)} %is-finite_select_fusion.3, ...), kind=kLoop, calls=%fused_computation.16 | loop fusion | flops 20967416 | bytes 17858592 | tf_op jit(solution)/shard_map/reduce_max | solution.py:65
  88.4 6.6 %collective-permute-done = bf16[1024,768]{1,0:T(8,128)(2,1)} collective-permute-done((bf16[1024,768]{1,0:T(8,128)(2,1)}, bf16[1024,768]{1,0:T(8,128)(2,1)}, u32[]{:S(2)}, u32[]{:S(2)}) %collective-permute-start) | collective-permute-done | bytes 1572896 | tf_op jit(solution)/shard_map/ppermute | solution.py:28
  95.0 1.7 copy.31
  99.9 4.6 %fusion.10 = (f32[4]{0:T(128)S(1)}, f32[4,512]{1,0:T(4,128)S(1)}, f32[4,512]{1,0:T(4,128)S(1)}, f32[4]{0:T(128)S(1)}) fusion(f32[4,512,1024]{2,1,0:T(8,128)S(1)} %get-tuple-element.32, pred[]{:T(512)S(6)} %gt.4, f32[4,512]{1,0:T(4,128)S(1)} %is-finite_select_fusion.4, f32[4,512]{1,0:T(4,128)S(1)} %is-finite_select_fusion, ...), kind=kLoop, calls=%fused_computation.18 | loop fusion | flops 20967416 | bytes 16810016 | tf_op jit(solution)/shard_map/reduce_max | solution.py:96
  104.5 5.4 %collective-permute-start.1 = (bf16[1024,512]{0,1:T(8,128)(2,1)S(1)}, bf16[1024,512]{0,1:T(8,128)(2,1)}, u32[]{:S(2)}, u32[]{:S(2)}) collective-permute-start(bf16[1024,512]{0,1:T(8,128)(2,1)S(1)} %copy-done.9), channel_id=1, source_target_pairs={{0,8},{8,16},{16,24},{1,9},{9,17},{17,25},{2,10},{10,18},{18,26},{... | collective-permute-start | bytes 3145736 | tf_op jit(solution)/shard_map/ppermute | solution.py:28
  109.8 26.2 %pmax.7 = f32[4]{0:T(128)S(1)} all-reduce(f32[4]{0:T(128)S(1)} %maximum_maximum_fusion), channel_id=1, replica_groups=mesh['ctx'=4,'head'=4,'fsdp'=2] {'ctx'}, use_global_device_ids=true, to_apply=%region_12.13 | all-reduce | flops 4 | bytes 32 | tf_op jit(solution)/shard_map/pmax | solution.py:103
  136.4 12.0 %all-reduce.1 = f32[32]{0:T(128)S(1)} all-reduce(f32[32]{0:T(128)S(1)} %reshape.100), channel_id=1, replica_groups=mesh['ctx'=4,'head'=4,'fsdp'=2] {'head','fsdp'}, use_global_device_ids=true, to_apply=%add | all-reduce | flops 32 | bytes 256
  148.9 4.8 %fusion.49 = f32[512,4,128]{0,2,1:T(8,128)S(1)} fusion(bf16[1024,4,128]{0,2,1:T(8,128)(2,1)S(1)} %copy-done.8, f32[4,512,1024]{2,1,0:T(8,128)} %copy-done.4, f32[4,512]{1,0:T(4,128)S(1)} %is-finite_select_fusion.7, pred[512,1024]{1,0:T(8,128)(4,1)S(1)} %copy-done.6, f32[512,4]{0,1:T(4,128)S(1)} %get-tuple-element.15), kind=kOutput, calls=%fused_computation.41 | convolution fusion | flops 545521664 | bytes 11026432 | tf_op jit(solution)/shard_map/htu,uhd->thd/dot_general | solution.py:38
  154.7 3.5 %divide_convert_fusion.1 = bf16[512,4,128]{0,2,1:T(8,128)(2,1)S(1)} fusion(f32[512,4,128]{0,2,1:T(8,128)S(1)} %fusion.49, bf16[1024,4,128]{0,2,1:T(8,128)(2,1)} %bitcast.15, f32[4,512,1024]{2,1,0:T(8,128)S(1)} %copy-done.2, f32[4,512]{1,0:T(4,128)S(1)} %is-finite_select_fusion.4, pred[]{:T(512)S(6)} %gt.4, f32[512,4]{0,1:T(4,128)S(1)} %get-tuple-element.13, ...), kind=kOutput, calls=%fused_computation.48 | convolution fusion | flops 546308096 | bytes 11034625 | tf_op jit(solution)/shard_map/htu,uhd->thd/dot_general | solution.py:38
  158.4 4.7 %fusion.46 = f32[512,4,128]{0,2,1:T(8,128)S(1)} fusion(bf16[1024,4,128]{0,2,1:T(8,128)(2,1)S(1)} %copy-done.8, f32[4,512,1024]{2,1,0:T(8,128)} %copy-done.3, f32[4,512]{1,0:T(4,128)S(1)} %is-finite_select_fusion.3, pred[512,1024]{1,0:T(8,128)(4,1)S(1)} %copy-done.5, f32[512,4]{0,1:T(4,128)S(1)} %get-tuple-element.18), kind=kOutput, calls=%fused_computation.40 | convolution fusion | flops 545521664 | bytes 11026432 | tf_op jit(solution)/shard_map/htu,uhd->thd/dot_general | solution.py:38
  163.1 5.8 %divide_convert_fusion = bf16[512,4,128]{0,2,1:T(8,128)(2,1)S(1)} fusion(f32[512,4,128]{0,2,1:T(8,128)S(1)} %fusion.46, bf16[1024,4,128]{0,2,1:T(8,128)(2,1)} %bitcast.15, f32[4,512,1024]{2,1,0:T(8,128)} %copy-done, f32[4,512]{1,0:T(4,128)S(1)} %is-finite_select_fusion, pred[]{:T(512)S(6)} %gt.4, f32[512,4]{0,1:T(4,128)S(1)} %get-tuple-element.16, ...), kind=kOutput, calls=%fused_computation.47 | convolution fusion | flops 546308096 | bytes 11034625 | tf_op jit(solution)/shard_map/htu,uhd->thd/dot_general | solution.py:38
  (73 shorter events, 24.1 us)
Async XLA Ops:
  1.9 46.6 %copy-start.15 = (u32[32]{0:T(128)S(1)}, u32[32]{0:T(128)}, u32[]{:S(2)}) copy-start(u32[32]{0:T(128)} %constant.30) | copy-start | bytes 388
  3.0 18.8 %all-to-all-start = ((bf16[4,256,512]{2,1,0:T(8,128)(2,1)}), bf16[4,256,512]{2,1,0:T(8,128)(2,1)S(1)}, u32[]{:S(2)}, u32[]{:S(2)}) async-start(bf16[4,256,512]{2,1,0:T(8,128)(2,1)} %pad_maximum_fusion), calls=%async_computation | async-start | bytes 2097152 | tf_op jit(solution)/shard_map/all_to_all | solution.py:15
  21.8 22.3 %all-to-all-start.2 = ((bf16[256,4,768]{0,2,1:T(8,128)(2,1)}), bf16[256,4,768]{0,2,1:T(8,128)(2,1)S(1)}, u32[]{:S(2)}, u32[]{:S(2)}) async-start(bf16[256,4,768]{0,2,1:T(8,128)(2,1)} %bitcast.117), calls=%async_computation.2 | async-start | bytes 3145728 | tf_op jit(solution)/shard_map/all_to_all | solution.py:71
  44.1 23.2 %all-to-all-start.1 = ((bf16[256,4,768]{0,2,1:T(8,128)(2,1)}), bf16[256,4,768]{0,2,1:T(8,128)(2,1)}, u32[]{:S(2)}, u32[]{:S(2)}) async-start(bf16[256,4,768]{0,2,1:T(8,128)(2,1)} %bitcast.116), calls=%async_computation.1 | async-start | bytes 3145728 | tf_op jit(solution)/shard_map/all_to_all | solution.py:70
  58.3 36.7 %collective-permute-start = (bf16[1024,768]{1,0:T(8,128)(2,1)}, bf16[1024,768]{1,0:T(8,128)(2,1)}, u32[]{:S(2)}, u32[]{:S(2)}) collective-permute-start(bf16[1024,768]{1,0:T(8,128)(2,1)} %bitcast.11), channel_id=1, source_target_pairs={{0,8},{8,16},{16,24},{1,9},{9,17},{17,25},{2,10},{10,18},{18,26},{... | collective-permute-start | bytes 4718600 | tf_op jit(solution)/shard_map/ppermute | solution.py:28
  74.4 6.3 %copy-start.6 = (pred[512,1024]{1,0:T(8,128)(4,1)S(1)}, pred[512,1024]{1,0:T(8,128)(4,1)}, u32[]{:S(2)}) copy-start(pred[512,1024]{1,0:T(8,128)(4,1)} %iota_compare_fusion.1) | copy-start | bytes 1572868
  76.9 3.8 %copy-start.7 = (bf16[1024,4,192]{0,2,1:T(8,128)(2,1)S(1)}, bf16[1024,4,192]{0,2,1:T(8,128)(2,1)}, u32[]{:S(2)}) copy-start(bf16[1024,4,192]{0,2,1:T(8,128)(2,1)} %reshape.95) | copy-start | bytes 4718596
  76.9 3.8 %copy-start.11 = (bf16[512,4,192]{0,2,1:T(8,128)(2,1)S(1)}, bf16[512,4,192]{0,2,1:T(8,128)(2,1)}, u32[]{:S(2)}) copy-start(bf16[512,4,192]{0,2,1:T(8,128)(2,1)} %slice.15) | copy-start | bytes 2359300
  80.8 7.6 %copy-start.3 = (f32[4,512,1024]{2,1,0:T(8,128)}, f32[4,512,1024]{2,1,0:T(8,128)S(1)}, u32[]{:S(2)}) copy-start(f32[4,512,1024]{2,1,0:T(8,128)S(1)} %get-tuple-element.26) | copy-start | bytes 25165828
  80.8 2.0 %copy-start.5 = (pred[512,1024]{1,0:T(8,128)(4,1)S(1)}, pred[512,1024]{1,0:T(8,128)(4,1)}, u32[]{:S(2)}) copy-start(pred[512,1024]{1,0:T(8,128)(4,1)} %iota_compare_fusion) | copy-start | bytes 1572868
  82.7 5.7 %copy-start.4 = (f32[4,512,1024]{2,1,0:T(8,128)}, f32[4,512,1024]{2,1,0:T(8,128)S(1)}, u32[]{:S(2)}) copy-start(f32[4,512,1024]{2,1,0:T(8,128)S(1)} %get-tuple-element.30) | copy-start | bytes 25165828
  82.8 14.0 %copy-start.10 = (bf16[512,4,192]{0,2,1:T(8,128)(2,1)S(1)}, bf16[512,4,192]{0,2,1:T(8,128)(2,1)}, u32[]{:S(2)}) copy-start(bf16[512,4,192]{0,2,1:T(8,128)(2,1)} %slice.17) | copy-start | bytes 2359300
  96.7 1.5 copy-start.12
  98.3 6.1 %copy-start = (f32[4,512,1024]{2,1,0:T(8,128)}, f32[4,512,1024]{2,1,0:T(8,128)S(1)}, u32[]{:S(2)}) copy-start(f32[4,512,1024]{2,1,0:T(8,128)S(1)} %get-tuple-element.28) | copy-start | bytes 25165828
  99.8 4.6 %copy-start.1 = (f32[4,512,1024]{2,1,0:T(8,128)}, f32[4,512,1024]{2,1,0:T(8,128)S(1)}, u32[]{:S(2)}) copy-start(f32[4,512,1024]{2,1,0:T(8,128)S(1)} %get-tuple-element.32) | copy-start | bytes 25165828
  99.8 4.6 %copy-start.9 = (bf16[1024,512]{0,1:T(8,128)(2,1)S(1)}, bf16[1024,512]{0,1:T(8,128)(2,1)}, u32[]{:S(2)}) copy-start(bf16[1024,512]{0,1:T(8,128)(2,1)} %copy.32) | copy-start | bytes 3145732
  99.8 49.0 %copy-start.8 = (bf16[1024,4,128]{0,2,1:T(8,128)(2,1)S(1)}, bf16[1024,4,128]{0,2,1:T(8,128)(2,1)}, u32[]{:S(2)}) copy-start(bf16[1024,4,128]{0,2,1:T(8,128)(2,1)} %copy.37) | copy-start | bytes 3145732
  104.5 49.2 %collective-permute-start.1 = (bf16[1024,512]{0,1:T(8,128)(2,1)S(1)}, bf16[1024,512]{0,1:T(8,128)(2,1)}, u32[]{:S(2)}, u32[]{:S(2)}) collective-permute-start(bf16[1024,512]{0,1:T(8,128)(2,1)S(1)} %copy-done.9), channel_id=1, source_target_pairs={{0,8},{8,16},{16,24},{1,9},{9,17},{17,25},{2,10},{10,18},{18,26},{... | collective-permute-start | bytes 3145736 | tf_op jit(solution)/shard_map/ppermute | solution.py:28
  148.8 5.8 %copy-start.2 = (f32[4,512,1024]{2,1,0:T(8,128)S(1)}, f32[4,512,1024]{2,1,0:T(8,128)}, u32[]{:S(2)}) copy-start(f32[4,512,1024]{2,1,0:T(8,128)} %copy-done.1) | copy-start | bytes 25165828
  163.1 6.1 %copy-start.13 = (bf16[192,1536]{1,0:T(8,128)(2,1)S(1)}, bf16[192,1536]{1,0:T(8,128)(2,1)}, u32[]{:S(2)}) copy-start(bf16[192,1536]{1,0:T(8,128)(2,1)} %param.8) | copy-start | bytes 1769476
  163.1 7.0 %copy-start.14 = (bf16[64,1024]{1,0:T(8,128)(2,1)S(1)}, bf16[64,1024]{1,0:T(8,128)(2,1)}, u32[]{:S(2)}) copy-start(bf16[64,1024]{1,0:T(8,128)(2,1)} %param.9) | copy-start | bytes 393220
